TPU v7x, 32 devices: a whole 2x2x4 slice. The times are simulated.
32 devices in a mesh: dp: 4 (over z), ctx: 4 (over x, core), uly: 2 (over y).
Axes of the slice: x: 2, y: 2, z: 4, core: 2. Of those that a mesh axis runs over, the one named last changes fastest.
Arguments:
- queries: bfloat16 [4096, 4096], P(('dp', 'ctx', 'uly')), parts along dimension 0, may hold values from -130 to 130
- keys: bfloat16 [4096, 1024], P(('dp', 'ctx', 'uly')), parts along dimension 0, may hold values from -6.5 to 6.5
- values: bfloat16 [4096, 1024], P(('dp', 'ctx', 'uly')), parts along dimension 0, may hold values from -6 to 6
- d_out: bfloat16 [4096, 4096], P(('dp', 'ctx', 'uly')), parts along dimension 0, may hold values from -96 to 96
- rand_blocks: int32 [32, 3], P('dp'), parts along dimension 0, may hold values from 0 to 7, as said below
Outputs:
- d_queries: bfloat16 [4096, 4096], P(('dp', 'ctx', 'uly')), parts along dimension 0
- d_keys: bfloat16 [4096, 1024], P(('dp', 'ctx', 'uly')), parts along dimension 0
- d_values: bfloat16 [4096, 1024], P(('dp', 'ctx', 'uly')), parts along dimension 0
There are 4 independent parts, one for each index of `dp`. A program takes and returns all parts, laid end to end along the dimension named above; each array names one. Nothing has to cross between parts.
Inputs may be any that keep to these rules, and one draw needn't show every extreme that they name: `rand_blocks`: for every group of 2 consecutive query blocks, the entries of its lists (window, random) that name blocks of one other group of 2 number at most 2, and at most 4 when the 2 global blocks are counted once each; both bounds are reached in every draw.
All inputs are finite; a program needn't handle non-finite values.
Results may differ from a plain program's by a relative error of at most 0.005.
Values may be sent and summed in bfloat16 or wider, within the bound.
No kernel may reach another device: no remote copies, remote signals or barrier semaphores. Data moves between devices by JAX's collectives and lax.ppermute only.
A program may use at most 128 MiB of HBM per device.

v0:
```python
from functools import partial
import jax
import jax.numpy as jnp
from jax import lax
from jax.sharding import PartitionSpec as P

HEAD_DIM = 128
BLOCK = 128
WINDOW = 3
GLOBALS = 2
RANDOMS = 3
ENTRIES = 8
GROUP = 4


def listed_blocks(rand_blocks):
    total = rand_blocks.shape[0]
    block_ids = jnp.arange(total, dtype=jnp.int32)
    window_part = (
        block_ids[:, None] + jnp.arange(WINDOW, dtype=jnp.int32)[None, :] - WINDOW // 2
    ) % total
    global_part = jnp.broadcast_to(jnp.arange(GLOBALS, dtype=jnp.int32)[None, :], (total, GLOBALS))
    return jnp.concatenate([window_part, global_part, rand_blocks], axis=1)


def block_backward(sources, softmax_scale, inputs):
    query_blk, dout_blk, source_rows = inputs
    picked = jnp.take(sources, source_rows, axis=0)
    kv_width = picked.shape[-1] // 2
    kv_count = kv_width // HEAD_DIM
    key_sel = picked[..., :kv_width].reshape(ENTRIES, BLOCK, kv_count, HEAD_DIM)
    value_sel = picked[..., kv_width:].reshape(ENTRIES, BLOCK, kv_count, HEAD_DIM)
    query_four = query_blk.reshape(BLOCK, kv_count, GROUP, HEAD_DIM)
    dout_four = dout_blk.reshape(BLOCK, kv_count, GROUP, HEAD_DIM)
    scores = jnp.einsum("tkgd,eskd->kgtes", query_four, key_sel, preferred_element_type=jnp.float32)
    scores = scores.reshape(kv_count, GROUP, BLOCK, ENTRIES * BLOCK) * softmax_scale
    row_max = jnp.max(scores, axis=-1, keepdims=True)
    exp_scores = jnp.exp(scores - row_max)
    prob_rows = exp_scores / jnp.sum(exp_scores, axis=-1, keepdims=True)
    grad_probs = jnp.einsum(
        "tkgd,eskd->kgtes", dout_four, value_sel, preferred_element_type=jnp.float32
    )
    grad_probs = grad_probs.reshape(kv_count, GROUP, BLOCK, ENTRIES * BLOCK)
    row_delta = jnp.sum(prob_rows * grad_probs, axis=-1, keepdims=True)
    grad_scores = (
        (prob_rows * (grad_probs - row_delta))
        .astype(jnp.bfloat16)
        .reshape(kv_count, GROUP, BLOCK, ENTRIES, BLOCK)
    )
    probs_low = prob_rows.astype(jnp.bfloat16).reshape(kv_count, GROUP, BLOCK, ENTRIES, BLOCK)
    grad_values = jnp.einsum(
        "kgtes,tkgd->eskd", probs_low, dout_four, preferred_element_type=jnp.float32
    )
    grad_keys = (
        jnp.einsum("kgtes,tkgd->eskd", grad_scores, query_four, preferred_element_type=jnp.float32)
        * softmax_scale
    )
    grad_query = (
        jnp.einsum("kgtes,eskd->tkgd", grad_scores, key_sel, preferred_element_type=jnp.float32)
        * softmax_scale
    )
    partials = jnp.concatenate(
        [
            grad_keys.reshape(ENTRIES, BLOCK, kv_width),
            grad_values.reshape(ENTRIES, BLOCK, kv_width),
        ],
        axis=-1,
    )
    return (partials, grad_query.reshape(BLOCK, kv_count * GROUP * HEAD_DIM))


def per_device(queries, keys, values, d_out, rand_blocks):
    softmax_scale = HEAD_DIM ** (-0.5)
    groups = lax.axis_size("ctx")
    my_group = lax.axis_index("ctx")
    queries_here, dout_here, keys_here, values_here = (
        lax.all_to_all(queries, "uly", split_axis=1, concat_axis=0, tiled=True),
        lax.all_to_all(d_out, "uly", split_axis=1, concat_axis=0, tiled=True),
        lax.all_to_all(keys, "uly", split_axis=1, concat_axis=0, tiled=True),
        lax.all_to_all(values, "uly", split_axis=1, concat_axis=0, tiled=True),
    )
    tokens_here = keys_here.shape[0]
    per_group = tokens_here // BLOCK
    kv_width = keys_here.shape[1]
    local_blocks = jnp.concatenate([keys_here, values_here], axis=1).reshape(
        per_group, BLOCK, 2 * kv_width
    )
    listed = listed_blocks(rand_blocks)
    owners = listed // per_group
    offsets = listed % per_group
    requester = (jnp.arange(listed.shape[0], dtype=jnp.int32) // per_group)[:, None]
    entry_ids = jnp.arange(ENTRIES, dtype=jnp.int32)
    is_global = (entry_ids >= WINDOW) & (entry_ids < WINDOW + GLOBALS)
    entry_global = jnp.tile(is_global, per_group)
    global_slot = jnp.tile(entry_ids - WINDOW, per_group)
    rand_capacity = per_group * RANDOMS // groups + 1
    remote = owners != requester
    capacity = rand_capacity + GLOBALS
    lead_slots = GLOBALS
    owners = owners.reshape(groups, per_group * ENTRIES)
    offsets = offsets.reshape(groups, per_group * ENTRIES)
    remote = remote.reshape(groups, per_group * ENTRIES)
    counted = remote & jnp.logical_not(entry_global)[None, :]
    owner_hot = (
        (owners[:, :, None] == jnp.arange(groups, dtype=jnp.int32)[None, None, :])
        & counted[:, :, None]
    ).astype(jnp.int32)
    rand_slot = jnp.sum((jnp.cumsum(owner_hot, axis=1) - 1) * owner_hot, axis=2) + lead_slots
    slot_index = jnp.where(entry_global[None, :], global_slot[None, :], rand_slot)
    for_me = remote & (owners == my_group)
    slot_match = (
        slot_index[:, :, None, None] == jnp.arange(capacity, dtype=jnp.int32)[None, None, :, None]
    )
    block_match = (
        offsets[:, :, None, None] == jnp.arange(per_group, dtype=jnp.int32)[None, None, None, :]
    )
    slot_picker = jnp.minimum(
        jnp.sum((for_me[:, :, None, None] & slot_match & block_match).astype(jnp.int32), axis=1), 1
    )
    outgoing = jnp.einsum(
        "csb,bxd->csxd",
        slot_picker.astype(jnp.bfloat16),
        local_blocks,
        preferred_element_type=jnp.float32,
    ).astype(jnp.bfloat16)
    incoming = lax.all_to_all(outgoing, "ctx", split_axis=0, concat_axis=0, tiled=True)
    my_owner = lax.dynamic_index_in_dim(owners, my_group, 0, keepdims=False)
    my_slot = lax.dynamic_index_in_dim(slot_index, my_group, 0, keepdims=False)
    my_offset = lax.dynamic_index_in_dim(offsets, my_group, 0, keepdims=False)
    my_remote = lax.dynamic_index_in_dim(remote, my_group, 0, keepdims=False)
    source_rows = jnp.where(my_remote, per_group + my_owner * capacity + my_slot, my_offset)
    pieces = [local_blocks, incoming.reshape(groups * capacity, BLOCK, 2 * kv_width)]
    sources = jnp.concatenate(pieces, axis=0)
    source_count = sources.shape[0]
    query_blocks = queries_here.reshape(per_group, BLOCK, queries_here.shape[1])
    dout_blocks = dout_here.reshape(per_group, BLOCK, dout_here.shape[1])
    partials, grad_query = lax.map(
        partial(block_backward, sources, softmax_scale),
        (query_blocks, dout_blocks, source_rows.reshape(per_group, ENTRIES)),
    )
    source_hot = (
        source_rows[:, None] == jnp.arange(source_count, dtype=jnp.int32)[None, :]
    ).astype(jnp.float32)
    source_grads = jnp.einsum(
        "ms,mxd->sxd",
        source_hot,
        partials.reshape(per_group * ENTRIES, BLOCK, 2 * kv_width),
        precision=lax.Precision.HIGHEST,
    )
    own_grads = source_grads[:per_group]
    sent_grads = source_grads[per_group : per_group + groups * capacity].reshape(
        groups, capacity, BLOCK, 2 * kv_width
    )
    returned = lax.all_to_all(sent_grads, "ctx", split_axis=0, concat_axis=0, tiled=True)
    own_grads = own_grads + jnp.einsum(
        "csb,csxd->bxd", slot_picker.astype(jnp.float32), returned, precision=lax.Precision.HIGHEST
    )
    query_grads = grad_query.reshape(tokens_here, queries_here.shape[1]).astype(jnp.bfloat16)
    key_grads = own_grads[..., :kv_width].reshape(tokens_here, kv_width).astype(jnp.bfloat16)
    value_grads = own_grads[..., kv_width:].reshape(tokens_here, kv_width).astype(jnp.bfloat16)
    d_queries, d_keys, d_values = (
        lax.all_to_all(query_grads, "uly", split_axis=0, concat_axis=1, tiled=True),
        lax.all_to_all(key_grads, "uly", split_axis=0, concat_axis=1, tiled=True),
        lax.all_to_all(value_grads, "uly", split_axis=0, concat_axis=1, tiled=True),
    )
    return (d_queries, d_keys, d_values)


def solution(mesh):
    in_specs = (
        P(("dp", "ctx", "uly"), None),
        P(("dp", "ctx", "uly"), None),
        P(("dp", "ctx", "uly"), None),
        P(("dp", "ctx", "uly"), None),
        P("dp", None),
    )
    out_specs = (
        P(("dp", "ctx", "uly"), None),
        P(("dp", "ctx", "uly"), None),
        P(("dp", "ctx", "uly"), None),
    )
    return jax.shard_map(
        per_device, mesh=mesh, in_specs=in_specs, out_specs=out_specs, check_vma=False
    )
```

profile of v0, /device:TPU:0, one launch (start us, length us, event | category | flops | bytes accessed | tf_op | source)
XLA Modules:
  0.0 362.4 jit_solution(10996990037546857192)
XLA Ops:
  2.6 4.2 %all-to-all-start.2 = ((bf16[128,2,512]{2,0,1:T(8,128)(2,1)}), bf16[128,2,512]{2,0,1:T(8,128)(2,1)S(1)}, u32[]{:S(2)}, u32[]{:S(2)}) async-start(bf16[128,2,512]{2,0,1:T(8,128)(2,1)} %copy.130), calls=%async_computation.2 | async-start | bytes 524288 | tf_op jit(solution)/shard_map/all_to_all | solution.py:80
  10.5 2.3 copy.124
  12.7 3.5 all-to-all-start.1
  16.2 5.8 %all-to-all-done.1 = bf16[128,2,512]{2,0,1:T(8,128)(2,1)S(1)} async-done(((bf16[128,2,512]{2,0,1:T(8,128)(2,1)}), bf16[128,2,512]{2,0,1:T(8,128)(2,1)S(1)}, u32[]{:S(2)}, u32[]{:S(2)}) %all-to-all-start.1) | async-done | bytes 262176 | tf_op jit(solution)/shard_map/all_to_all | solution.py:79
  22.1 4.4 %all-to-all-start = ((bf16[128,2,2048]{0,2,1:T(8,128)(2,1)}), bf16[128,2,2048]{0,2,1:T(8,128)(2,1)}, u32[]{:S(2)}, u32[]{:S(2)}) async-start(bf16[128,2,2048]{0,2,1:T(8,128)(2,1)} %bitcast.31), calls=%async_computation | async-start | bytes 2097152 | tf_op jit(solution)/shard_map/all_to_all | solution.py:77
  27.4 4.4 %convolution_convert_fusion = bf16[4,4,128,1024]{3,1,2,0:T(4,128)(2,1)} fusion(s32[4,4,2]{1,2,0:T(2,128)S(1)} %convert_reduce_fusion, bf16[2,128,512]{2,0,1:T(2,128)(2,1)S(1)} %bitcast.211, bf16[2,128,512]{2,0,1:T(2,128)(2,1)S(1)} %bitcast.213), kind=kOutput, calls=%fused_computation.38 | convolution fusion | flops 11534400 | bytes 4718720 | tf_op jit(solution)/shard_map/csb,bxd->csxd/dot_general | solution.py:120
  31.8 8.1 %all-to-all-done = bf16[128,2,2048]{0,2,1:T(8,128)(2,1)} async-done(((bf16[128,2,2048]{0,2,1:T(8,128)(2,1)}), bf16[128,2,2048]{0,2,1:T(8,128)(2,1)}, u32[]{:S(2)}, u32[]{:S(2)}) %all-to-all-start) | async-done | bytes 1048608 | tf_op jit(solution)/shard_map/all_to_all | solution.py:77
  39.9 4.9 %all-to-all-start.3 = ((bf16[4,4,128,1024]{3,1,2,0:T(4,128)(2,1)}), bf16[4,4,128,1024]{3,1,2,0:T(4,128)(2,1)}, u32[]{:S(2)}, u32[]{:S(2)}) async-start(bf16[4,4,128,1024]{3,1,2,0:T(4,128)(2,1)} %convolution_convert_fusion), calls=%async_computation.3 | async-start | bytes 8388608 | tf_op jit(solution)/shard_map/all_to_all | solution.py:126
  44.9 1.3 copy.134
  46.2 46.9 %all-to-all-done.3 = bf16[4,4,128,1024]{3,1,2,0:T(4,128)(2,1)} async-done(((bf16[4,4,128,1024]{3,1,2,0:T(4,128)(2,1)}), bf16[4,4,128,1024]{3,1,2,0:T(4,128)(2,1)}, u32[]{:S(2)}, u32[]{:S(2)}) %all-to-all-start.3) | async-done | bytes 4194336 | tf_op jit(solution)/shard_map/all_to_all | solution.py:126
  93.1 4.4 %all-to-all-start.4 = ((bf16[128,2,2048]{0,2,1:T(8,128)(2,1)}), bf16[128,2,2048]{0,2,1:T(8,128)(2,1)}, u32[]{:S(2)}, u32[]{:S(2)}) async-start(bf16[128,2,2048]{0,2,1:T(8,128)(2,1)} %bitcast.41), calls=%async_computation.4 | async-start | bytes 2097152 | tf_op jit(solution)/shard_map/all_to_all | solution.py:78
  99.9 3.6 %copy.132 = bf16[4,4,128,1024]{3,2,1,0:T(8,128)(2,1)S(1)} copy(bf16[4,4,128,1024]{3,1,2,0:T(4,128)(2,1)} %all-to-all-done.3) | data formatting | bytes 8388608 | tf_op jit(solution)/shard_map/all_to_all | solution.py:126
  103.6 2.5 pad_maximum_fusion
  106.1 5.2 %all-to-all-done.4 = bf16[128,2,2048]{0,2,1:T(8,128)(2,1)} async-done(((bf16[128,2,2048]{0,2,1:T(8,128)(2,1)}), bf16[128,2,2048]{0,2,1:T(8,128)(2,1)}, u32[]{:S(2)}, u32[]{:S(2)}) %all-to-all-start.4) | async-done | bytes 1048608 | tf_op jit(solution)/shard_map/all_to_all | solution.py:78
  111.3 65.8 %while.12 = (s32[]{:T(128)}, f32[2,8,128,1024]{2,3,1,0:T(8,128)}, bf16[2,128,2048]{1,2,0:T(8,128)(2,1)}, bf16[2,128,2048]{1,2,0:T(8,128)(2,1)}, s32[2,8]{1,0:T(2...) while((s32[]{:T(128)}, f32[2,8,128,1024]{2,3,1,0:T(8,128)}, ...), condition=%wide.region_7.8_spmd, body=%wide.region_3.7_spmd.sunk | while | flops 2729438208 | bytes 243889072 | solution.py:137
  111.3 3.0 gather_fusion
  115.9 1.6 copy.204
  118.8 1.3 bitcast_reduce_fusion.2
  120.1 3.2 copy-done
  123.4 1.4 fusion.90
  126.1 5.3 %fusion.92 = (f32[4,4,128]{2,1,0:T(4,128)S(1)}, f32[4,8,128,128,4]{3,2,4,1,0:T(8,128)S(1)}) fusion(f32[4,4,128]{2,1,0:T(4,128)S(1)} %fusion.90, f32[4,4,128]{2,1,0:T(4,128)S(1)} %get-tuple-element.135, f32[4,8,128,128,4]{3,2,4,1,0:T(8,128)} %copy-done, bf16[128,4,4,128,1]{0,3,2,4,1:T(8,128)(2,1)S(1)} %bitcast.200, ...), kind=kOutput, calls=%fused_computation.3.clone.1 | convolution fusion | flops 547354624 | bytes 18374656 | tf_op jit(solution)/shard_map/while/body/eval_jaxpr/tkgd,eskd->kgtes/dot_general | solution.py:40
  132.2 2.4 fusion.93
  134.6 1.5 fusion.94
  136.3 2.2 fusion.91
  140.9 2.5 copy-done.3
  144.2 3.0 gather_fusion
  148.8 1.6 copy.204
  153.0 3.2 copy-done
  156.3 1.4 fusion.90
  159.0 5.3 %fusion.92 = (f32[4,4,128]{2,1,0:T(4,128)S(1)}, f32[4,8,128,128,4]{3,2,4,1,0:T(8,128)S(1)}) fusion(f32[4,4,128]{2,1,0:T(4,128)S(1)} %fusion.90, f32[4,4,128]{2,1,0:T(4,128)S(1)} %get-tuple-element.135, f32[4,8,128,128,4]{3,2,4,1,0:T(8,128)} %copy-done, bf16[128,4,4,128,1]{0,3,2,4,1:T(8,128)(2,1)S(1)} %bitcast.200, ...), kind=kOutput, calls=%fused_computation.3.clone.1 | convolution fusion | flops 547354624 | bytes 18374656 | tf_op jit(solution)/shard_map/while/body/eval_jaxpr/tkgd,eskd->kgtes/dot_general | solution.py:40
  165.1 2.4 fusion.93
  167.5 1.5 fusion.94
  169.2 2.2 fusion.91
  173.8 2.5 copy-done.3
  177.1 8.9 %copy.136 = f32[16,128,1024]{2,0,1:T(8,128)} copy(f32[16,128,1024]{1,2,0:T(8,128)} %bitcast.205) | data formatting | bytes 16777216 | tf_op jit(solution)/shard_map/reshape | solution.py:147
  186.0 9.6 %fusion.35 = f32[18,128,1024]{2,0,1:T(8,128)S(1)} fusion(f32[16,128,1024]{2,0,1:T(8,128)} %copy.136, s32[16]{0:T(128)S(1)} %bitcast.215), kind=kOutput, calls=%fused_computation.55 | convolution fusion | flops 452985120 | bytes 17825856 | tf_op jit(solution)/shard_map/ms,mxd->sxd/dot_general | solution.py:144
  195.6 4.5 %copy-done.2 = f32[18,128,1024]{2,0,1:T(8,128)} copy-done((f32[18,128,1024]{2,0,1:T(8,128)}, f32[18,128,1024]{2,0,1:T(8,128)S(1)}, u32[]{:S(2)}) %copy-start.2) | copy-done | bytes 9437208
  200.1 5.3 %slice.29 = f32[16,128,1024]{2,0,1:T(8,128)} slice(f32[18,128,1024]{2,0,1:T(8,128)S(1)} %fusion.35), slice={[2:18], [0:128], [0:1024]} | slice | bytes 16777216 | tf_op jit(solution)/shard_map/slice | solution.py:151
  205.4 9.8 %reshape.355 = f32[4,4,128,1024]{3,1,0,2:T(4,128)} reshape(f32[16,128,1024]{2,0,1:T(8,128)} %slice.29) | data formatting | bytes 16777216 | tf_op jit(solution)/shard_map/reshape | solution.py:151
  215.2 9.4 %copy.137 = f32[4,4,128,1024]{3,1,2,0:T(4,128)} copy(f32[4,4,128,1024]{3,1,0,2:T(4,128)} %reshape.355) | data formatting | bytes 16777216 | tf_op jit(solution)/shard_map/reshape | solution.py:151
  224.7 100.7 %all_to_all.122 = f32[4,4,128,1024]{3,1,2,0:T(4,128)} all-to-all(f32[4,4,128,1024]{3,1,2,0:T(4,128)} %copy.137), channel_id=1, replica_groups=mesh['dp'=4,'ctx'=4,'uly'=2] {'ctx'}, dimensions={0} | all-to-all | bytes 16777216 | tf_op jit(solution)/shard_map/all_to_all | solution.py:154
  325.3 3.6 all-to-all-start.5
  328.9 14.1 %fusion.29 = bf16[2,128,1024]{2,0,1:T(2,128)(2,1)S(1)} fusion(f32[4,4,128,1024]{3,1,2,0:T(4,128)} %all_to_all.122, f32[18,128,1024]{2,0,1:T(8,128)} %copy-done.2, s32[4,4,2]{1,2,0:T(2,128)S(1)} %copy-done.6), kind=kOutput, calls=%fused_computation.41 | convolution fusion | flops 50856000 | bytes 9961600 | tf_op jit(solution)/shard_map/csb,csxd->bxd/dot_general | solution.py:155
  344.1 3.4 all-to-all-start.7
  348.3 4.4 %all-to-all-done.7 = bf16[2,128,512]{2,1,0:T(8,128)(2,1)S(1)} async-done(((bf16[2,128,512]{2,1,0:T(8,128)(2,1)}), bf16[2,128,512]{2,1,0:T(8,128)(2,1)S(1)}, u32[]{:S(2)}, u32[]{:S(2)}) %all-to-all-start.7) | async-done | bytes 262176 | tf_op jit(solution)/shard_map/all_to_all | solution.py:163
  352.7 3.4 all-to-all-start.8
  356.2 1.3 copy.171
  358.5 2.8 all-to-all-done.8
  (98 shorter events, 30.6 us)
Async XLA Ops:
  2.6 10.1 %all-to-all-start.2 = ((bf16[128,2,512]{2,0,1:T(8,128)(2,1)}), bf16[128,2,512]{2,0,1:T(8,128)(2,1)S(1)}, u32[]{:S(2)}, u32[]{:S(2)}) async-start(bf16[128,2,512]{2,0,1:T(8,128)(2,1)} %copy.130), calls=%async_computation.2 | async-start | bytes 524288 | tf_op jit(solution)/shard_map/all_to_all | solution.py:80
  12.7 9.3 %all-to-all-start.1 = ((bf16[128,2,512]{2,0,1:T(8,128)(2,1)}), bf16[128,2,512]{2,0,1:T(8,128)(2,1)S(1)}, u32[]{:S(2)}, u32[]{:S(2)}) async-start(bf16[128,2,512]{2,0,1:T(8,128)(2,1)} %copy.127), calls=%async_computation.1 | async-start | bytes 524288 | tf_op jit(solution)/shard_map/all_to_all | solution.py:79
  16.2 28.6 %copy-start.4 = (bf16[128,4096]{1,0:T(8,128)(2,1)S(1)}, bf16[128,4096]{1,0:T(8,128)(2,1)}, u32[]{:S(2)}) copy-start(bf16[128,4096]{1,0:T(8,128)(2,1)} %param.10) | copy-start | bytes 3145732
  22.1 17.8 %all-to-all-start = ((bf16[128,2,2048]{0,2,1:T(8,128)(2,1)}), bf16[128,2,2048]{0,2,1:T(8,128)(2,1)}, u32[]{:S(2)}, u32[]{:S(2)}) async-start(bf16[128,2,2048]{0,2,1:T(8,128)(2,1)} %bitcast.31), calls=%async_computation | async-start | bytes 2097152 | tf_op jit(solution)/shard_map/all_to_all | solution.py:77
  26.7 0.6 copy-start.5
  39.9 53.2 %all-to-all-start.3 = ((bf16[4,4,128,1024]{3,1,2,0:T(4,128)(2,1)}), bf16[4,4,128,1024]{3,1,2,0:T(4,128)(2,1)}, u32[]{:S(2)}, u32[]{:S(2)}) async-start(bf16[4,4,128,1024]{3,1,2,0:T(4,128)(2,1)} %convolution_convert_fusion), calls=%async_computation.3 | async-start | bytes 8388608 | tf_op jit(solution)/shard_map/all_to_all | solution.py:126
  93.1 18.2 %all-to-all-start.4 = ((bf16[128,2,2048]{0,2,1:T(8,128)(2,1)}), bf16[128,2,2048]{0,2,1:T(8,128)(2,1)}, u32[]{:S(2)}, u32[]{:S(2)}) async-start(bf16[128,2,2048]{0,2,1:T(8,128)(2,1)} %bitcast.41), calls=%async_computation.4 | async-start | bytes 2097152 | tf_op jit(solution)/shard_map/all_to_all | solution.py:78
  120.1 3.2 copy-start
  126.1 6.1 %copy-start.1 = (f32[4,8,128,128,4]{3,2,4,1,0:T(8,128)S(1)}, f32[4,8,128,128,4]{3,2,4,1,0:T(8,128)}, u32[]{:S(2)}) copy-start(f32[4,8,128,128,4]{3,2,4,1,0:T(8,128)} %copy-done) | copy-start | bytes 25165828 | tf_op jit(solution)/shard_map/while
  136.1 2.6 slice-start
  136.3 3.4 slice-start.1
  140.1 3.2 copy-start.3
  153.0 3.2 copy-start
  159.0 6.1 %copy-start.1 = (f32[4,8,128,128,4]{3,2,4,1,0:T(8,128)S(1)}, f32[4,8,128,128,4]{3,2,4,1,0:T(8,128)}, u32[]{:S(2)}) copy-start(f32[4,8,128,128,4]{3,2,4,1,0:T(8,128)} %copy-done) | copy-start | bytes 25165828 | tf_op jit(solution)/shard_map/while
  169.0 2.6 slice-start
  169.2 3.4 slice-start.1
  173.0 3.2 copy-start.3
  177.1 8.9 %copy-start.7 = (s32[1,16]{1,0:T(1,128)S(1)}, s32[1,16]{1,0:T(1,128)}, u32[]{:S(2)}) copy-start(s32[1,16]{1,0:T(1,128)} %get-tuple-element.67) | copy-start | bytes 196
  195.6 4.5 %copy-start.2 = (f32[18,128,1024]{2,0,1:T(8,128)}, f32[18,128,1024]{2,0,1:T(8,128)S(1)}, u32[]{:S(2)}) copy-start(f32[18,128,1024]{2,0,1:T(8,128)S(1)} %fusion.35) | copy-start | bytes 28311556
  224.7 104.3 %copy-start.6 = (s32[4,4,2]{1,2,0:T(2,128)S(1)}, s32[4,4,2]{1,2,0:T(2,128)}, u32[]{:S(2)}) copy-start(s32[4,4,2]{1,2,0:T(2,128)} %copy-done.5) | copy-start | bytes 388
  325.3 18.8 %all-to-all-start.5 = ((bf16[2,128,2048]{1,2,0:T(8,128)(2,1)}), bf16[2,128,2048]{1,2,0:T(8,128)(2,1)S(1)}, u32[]{:S(2)}, u32[]{:S(2)}) async-start(bf16[2,128,2048]{1,2,0:T(8,128)(2,1)} %get-tuple-element.41), calls=%async_computation.5 | async-start | bytes 2097152 | tf_op jit(solution)/shard_map/all_to_all | solution.py:162
  344.1 8.6 %all-to-all-start.7 = ((bf16[2,128,512]{2,1,0:T(8,128)(2,1)}), bf16[2,128,512]{2,1,0:T(8,128)(2,1)S(1)}, u32[]{:S(2)}, u32[]{:S(2)}) async-start(bf16[2,128,512]{2,1,0:T(8,128)(2,1)} %copy.139), calls=%async_computation.7 | async-start | bytes 524288 | tf_op jit(solution)/shard_map/all_to_all | solution.py:163
  352.7 8.6 %all-to-all-start.8 = ((bf16[2,128,512]{2,1,0:T(8,128)(2,1)}), bf16[2,128,512]{2,1,0:T(8,128)(2,1)S(1)}, u32[]{:S(2)}, u32[]{:S(2)}) async-start(bf16[2,128,512]{2,1,0:T(8,128)(2,1)} %copy.141), calls=%async_computation.8 | async-start | bytes 524288 | tf_op jit(solution)/shard_map/all_to_all | solution.py:164
where the time goes:
time: 364 us; the launch traced here: 362 us
  blocking collectives  101 us (28%)
  local copies, waits for them, and re-layouts  90.3 us (25%)
  waiting for transfers between devices  73.3 us (20%)
  matrix products  50.2 us (14%)
  starting transfers between devices  31.9 us (9%)
  other arithmetic  14.7 us (4%)
    all_to_all x1, blocking collectives, per_device(): lax.all_to_all(sent_grads, 'ctx', split_axis=0, concat_axis=0, tiled=True)  101 us
    all_to_all x1, waiting for transfers between devices, per_device(): lax.all_to_all(outgoing, 'ctx', split_axis=0, concat_axis=0, tiled=True)  46.9 us
    reshape x2, local copies, waits for them, and re-layouts, per_device(): source_grads[per_group:per_group + groups * capacity]  19.2 us
    while x20, local copies, waits for them, and re-layouts  14.9 us
    dot_general x1, matrix products, per_device(): jnp.einsum('csb,csxd->bxd', slot_picker.astype(jnp.float32), returned, pr...  14.1 us
    unnamed x16, local copies, waits for them, and re-layouts  12.1 us
    dot_general x2, matrix products, block_backward(): jnp.einsum('tkgd,eskd->kgtes', dout_four, value_sel, preferred_element_ty...  10.7 us
    dot_general x1, matrix products, per_device(): jnp.einsum('ms,mxd->sxd', source_hot, partials.reshape(per_group * ENTRIE...  9.64 us
  transfers between devices with their start and end apart: 8, of which 6 were waited for; matrix products, arithmetic and copies ran while one was open for 11% of the time, Pallas kernels for 0%

commit v1 on v0

--- a/solution.py
+++ b/solution.py
@@ -123,7 +123,18 @@
         local_blocks,
         preferred_element_type=jnp.float32,
     ).astype(jnp.bfloat16)
-    incoming = lax.all_to_all(outgoing, "ctx", split_axis=0, concat_axis=0, tiled=True)
+    u1, f_next = (lax.axis_size("ctx"), lax.axis_index("ctx"))
+    ready = outgoing.shape[0] // u1
+    part_next = list(outgoing.shape)
+    part_next[0] = ready
+    b_now = part_next[0]
+    part_next[0] = b_now * u1
+    incoming = jnp.zeros(part_next, outgoing.dtype)
+    for i in range(u1):
+        val2 = lax.dynamic_slice_in_dim(outgoing, (f_next ^ i) * ready, ready, axis=0)
+        if i:
+            val2 = lax.ppermute(val2, axis_name="ctx", perm=[(num, num ^ i) for num in range(u1)])
+        incoming = lax.dynamic_update_slice_in_dim(incoming, val2, (f_next ^ i) * b_now, axis=0)
     my_owner = lax.dynamic_index_in_dim(owners, my_group, 0, keepdims=False)
     my_slot = lax.dynamic_index_in_dim(slot_index, my_group, 0, keepdims=False)
     my_offset = lax.dynamic_index_in_dim(offsets, my_group, 0, keepdims=False)

time: 364 us -> 335 us (0.920)
  waiting for transfers between devices: 73.3 us -> 35.4 us
  local copies, waits for them, and re-layouts: 90.3 us -> 104 us
    all_to_all x1 -> x0, waiting for transfers between devices: 46.9 us -> none  [per_device(): lax.all_to_all(outgoing, 'ctx', split_axis=0, concat_axis=0, tiled=True)]
    ppermute x0 -> x3, waiting for transfers between devices: none -> 14.1 us  [per_device(): lax.ppermute(val2, axis_name='ctx', perm=[(num, num ^ i) for num in range...]
    dynamic_update_slice x0 -> x4, local copies, waits for them, and re-layouts: none -> 10.4 us  [per_device(): lax.dynamic_update_slice_in_dim(incoming, val2, (f_next ^ i) * b_now, axi...]
    all_to_all x1, waiting for transfers between devices: 5.16 us -> 0.01 us  [per_device(): lax.all_to_all(d_out, 'uly', split_axis=1, concat_axis=0, tiled=True)]
    all_to_all x1 -> x0, starting transfers between devices: 4.93 us -> none  [per_device(): lax.all_to_all(outgoing, 'ctx', split_axis=0, concat_axis=0, tiled=True)]
    unnamed x16 -> x14, local copies, waits for them, and re-layouts: 12.1 us -> 13 us
  transfers between devices with their start and end apart: 8 -> 10, of which waited for: 6 -> 6; matrix products, arithmetic and copies ran while one was open for 11% -> 13% of each run, Pallas kernels for 0% -> 0%
where the time goes in v1:
time: 335 us; the launch traced here: 334 us
  local copies, waits for them, and re-layouts  104 us (31%)
  blocking collectives  101 us (30%)
  matrix products  48.7 us (15%)
  waiting for transfers between devices  35.4 us (11%)
  starting transfers between devices  28.9 us (9%)
  other arithmetic  14.6 us (4%)
    all_to_all x1, blocking collectives, per_device(): lax.all_to_all(sent_grads, 'ctx', split_axis=0, concat_axis=0, tiled=True)  101 us
    reshape x2, local copies, waits for them, and re-layouts, per_device(): source_grads[per_group:per_group + groups * capacity]  19.2 us
    while x20, local copies, waits for them, and re-layouts  14.9 us
    ppermute x3, waiting for transfers between devices, per_device(): lax.ppermute(val2, axis_name='ctx', perm=[(num, num ^ i) for num in range...  14.1 us
    dot_general x1, matrix products, per_device(): jnp.einsum('csb,csxd->bxd', slot_picker.astype(jnp.float32), returned, pr...  14.1 us
    unnamed x14, local copies, waits for them, and re-layouts  13 us
    dot_general x2, matrix products, block_backward(): jnp.einsum('tkgd,eskd->kgtes', dout_four, value_sel, preferred_element_ty...  10.7 us
    dynamic_update_slice x4, local copies, waits for them, and re-layouts, per_device(): lax.dynamic_update_slice_in_dim(incoming, val2, (f_next ^ i) * b_now, axi...  10.4 us
  transfers between devices with their start and end apart: 10, of which 6 were waited for; matrix products, arithmetic and copies ran while one was open for 13% of the time, Pallas kernels for 0%

profile of v1, /device:TPU:0, one launch (start us, length us, event | category | flops | bytes accessed | tf_op | source)
XLA Modules:
  0.0 333.7 jit_solution(9683864671505907872)
XLA Ops:
  2.6 4.2 %all-to-all-start.2 = ((bf16[128,2,512]{2,0,1:T(8,128)(2,1)}), bf16[128,2,512]{2,0,1:T(8,128)(2,1)S(1)}, u32[]{:S(2)}, u32[]{:S(2)}) async-start(bf16[128,2,512]{2,0,1:T(8,128)(2,1)} %copy.136), calls=%async_computation.2 | async-start | bytes 524288 | tf_op jit(solution)/shard_map/all_to_all | solution.py:80
  10.5 2.2 all-to-all-done.2
  12.7 3.4 %all-to-all-start.1 = ((bf16[128,2,512]{2,0,1:T(8,128)(2,1)}), bf16[128,2,512]{2,0,1:T(8,128)(2,1)S(1)}, u32[]{:S(2)}, u32[]{:S(2)}) async-start(bf16[128,2,512]{2,0,1:T(8,128)(2,1)} %copy.133), calls=%async_computation.1 | async-start | bytes 524288 | tf_op jit(solution)/shard_map/all_to_all | solution.py:79
  16.7 4.6 %all-to-all-done.1 = bf16[128,2,512]{2,0,1:T(8,128)(2,1)S(1)} async-done(((bf16[128,2,512]{2,0,1:T(8,128)(2,1)}), bf16[128,2,512]{2,0,1:T(8,128)(2,1)S(1)}, u32[]{:S(2)}, u32[]{:S(2)}) %all-to-all-start.1) | async-done | bytes 262176 | tf_op jit(solution)/shard_map/all_to_all | solution.py:79
  21.6 2.9 convolution_convert_fusion
  24.5 3.3 broadcast_in_dim.77
  27.8 2.9 constant_dynamic-slice_fusion.3
  30.7 1.7 collective-permute-start.1
  32.6 2.3 copy.130
  34.8 4.4 %all-to-all-start = ((bf16[128,2,2048]{0,2,1:T(8,128)(2,1)}), bf16[128,2,2048]{0,2,1:T(8,128)(2,1)}, u32[]{:S(2)}, u32[]{:S(2)}) async-start(bf16[128,2,2048]{0,2,1:T(8,128)(2,1)} %bitcast.31), calls=%async_computation | async-start | bytes 2097152 | tf_op jit(solution)/shard_map/all_to_all | solution.py:77
  41.0 2.3 copy.141
  43.9 2.6 constant_dynamic-update-slice_fusion.2
  46.5 7.2 %all-to-all-done = bf16[128,2,2048]{0,2,1:T(8,128)(2,1)} async-done(((bf16[128,2,2048]{0,2,1:T(8,128)(2,1)}), bf16[128,2,2048]{0,2,1:T(8,128)(2,1)}, u32[]{:S(2)}, u32[]{:S(2)}) %all-to-all-start) | async-done | bytes 1048608 | tf_op jit(solution)/shard_map/all_to_all | solution.py:77
  53.7 4.4 %all-to-all-start.3 = ((bf16[128,2,2048]{0,2,1:T(8,128)(2,1)}), bf16[128,2,2048]{0,2,1:T(8,128)(2,1)}, u32[]{:S(2)}, u32[]{:S(2)}) async-start(bf16[128,2,2048]{0,2,1:T(8,128)(2,1)} %bitcast.41), calls=%async_computation.3 | async-start | bytes 2097152 | tf_op jit(solution)/shard_map/all_to_all | solution.py:78
  58.1 2.6 constant_dynamic-update-slice_fusion.1
  60.7 3.6 %copy.138 = bf16[4,4,128,1024]{3,2,1,0:T(8,128)(2,1)S(1)} copy(bf16[4,4,128,1024]{3,1,2,0:T(4,128)(2,1)} %constant_dynamic-update-slice_fusion.1) | data formatting | bytes 8388608 | tf_op jit(solution)/shard_map/dynamic_update_slice | solution.py:137
  64.3 14.1 %collective-permute-done.2 = bf16[1,4,128,1024]{3,1,2,0:T(4,128)(2,1)} collective-permute-done((bf16[1,4,128,1024]{3,1,2,0:T(4,128)(2,1)S(1)}, bf16[1,4,128,1024]{3,1,2,0:T(4,128)(2,1)}, u32[]{:S(2)}, u32[]{:S(2)}) %collective-permute-start.2) | collective-permute-done | bytes 1048608 | tf_op jit(solution)/shard_map/ppermute | solution.py:136
  78.5 1.6 copy_dynamic-update-slice_fusion
  80.0 2.5 pad_maximum_fusion
  82.6 65.8 %while.12 = (s32[]{:T(128)}, f32[2,8,128,1024]{2,3,1,0:T(8,128)}, bf16[2,128,2048]{1,2,0:T(8,128)(2,1)}, bf16[2,128,2048]{1,2,0:T(8,128)(2,1)}, s32[2,8]{1,0:T(2...) while((s32[]{:T(128)}, f32[2,8,128,1024]{2,3,1,0:T(8,128)}, ...), condition=%wide.region_7.8_spmd, body=%wide.region_3.7_spmd.sunk | while | flops 2729438208 | bytes 243889072 | solution.py:148
  82.6 3.0 gather_fusion
  87.2 1.6 copy.212
  91.4 3.2 copy-done
  97.4 5.3 %fusion.94 = (f32[4,4,128]{2,1,0:T(4,128)S(1)}, f32[4,8,128,128,4]{3,2,4,1,0:T(8,128)S(1)}) fusion(f32[4,4,128]{2,1,0:T(4,128)S(1)} %fusion.92, f32[4,4,128]{2,1,0:T(4,128)S(1)} %get-tuple-element.139, f32[4,8,128,128,4]{3,2,4,1,0:T(8,128)} %copy-done, bf16[128,4,4,128,1]{0,3,2,4,1:T(8,128)(2,1)S(1)} %bitcast.200, ...), kind=kOutput, calls=%fused_computation.3.clone.1 | convolution fusion | flops 547354624 | bytes 18374656 | tf_op jit(solution)/shard_map/while/body/eval_jaxpr/tkgd,eskd->kgtes/dot_general | solution.py:40
  103.5 2.4 fusion.95
  107.6 2.2 fusion.93
  112.2 2.5 copy-done.3
  115.5 3.0 gather_fusion
  120.1 1.6 copy.212
  124.3 3.2 copy-done
  130.2 5.3 %fusion.94 = (f32[4,4,128]{2,1,0:T(4,128)S(1)}, f32[4,8,128,128,4]{3,2,4,1,0:T(8,128)S(1)}) fusion(f32[4,4,128]{2,1,0:T(4,128)S(1)} %fusion.92, f32[4,4,128]{2,1,0:T(4,128)S(1)} %get-tuple-element.139, f32[4,8,128,128,4]{3,2,4,1,0:T(8,128)} %copy-done, bf16[128,4,4,128,1]{0,3,2,4,1:T(8,128)(2,1)S(1)} %bitcast.200, ...), kind=kOutput, calls=%fused_computation.3.clone.1 | convolution fusion | flops 547354624 | bytes 18374656 | tf_op jit(solution)/shard_map/while/body/eval_jaxpr/tkgd,eskd->kgtes/dot_general | solution.py:40
  136.4 2.4 fusion.95
  138.8 1.5 fusion.96
  140.5 2.2 fusion.93
  145.1 2.5 copy-done.3
  148.4 8.9 %copy.143 = f32[16,128,1024]{2,0,1:T(8,128)} copy(f32[16,128,1024]{1,2,0:T(8,128)} %bitcast.205) | data formatting | bytes 16777216 | tf_op jit(solution)/shard_map/reshape | solution.py:158
  157.2 9.6 %fusion.35 = f32[18,128,1024]{2,0,1:T(8,128)S(1)} fusion(f32[16,128,1024]{2,0,1:T(8,128)} %copy.143, s32[16]{0:T(128)S(1)} %bitcast.215), kind=kOutput, calls=%fused_computation.57 | convolution fusion | flops 452985120 | bytes 17825856 | tf_op jit(solution)/shard_map/ms,mxd->sxd/dot_general | solution.py:155
  166.9 4.5 %copy-done.2 = f32[18,128,1024]{2,0,1:T(8,128)} copy-done((f32[18,128,1024]{2,0,1:T(8,128)}, f32[18,128,1024]{2,0,1:T(8,128)S(1)}, u32[]{:S(2)}) %copy-start.2) | copy-done | bytes 9437208
  171.4 5.3 %slice.29 = f32[16,128,1024]{2,0,1:T(8,128)} slice(f32[18,128,1024]{2,0,1:T(8,128)S(1)} %fusion.35), slice={[2:18], [0:128], [0:1024]} | slice | bytes 16777216 | tf_op jit(solution)/shard_map/slice | solution.py:162
  176.7 9.8 %reshape.355 = f32[4,4,128,1024]{3,1,0,2:T(4,128)} reshape(f32[16,128,1024]{2,0,1:T(8,128)} %slice.29) | data formatting | bytes 16777216 | tf_op jit(solution)/shard_map/reshape | solution.py:162
  186.5 9.4 %copy.144 = f32[4,4,128,1024]{3,1,2,0:T(4,128)} copy(f32[4,4,128,1024]{3,1,0,2:T(4,128)} %reshape.355) | data formatting | bytes 16777216 | tf_op jit(solution)/shard_map/reshape | solution.py:162
  196.0 100.7 %all_to_all.117 = f32[4,4,128,1024]{3,1,2,0:T(4,128)} all-to-all(f32[4,4,128,1024]{3,1,2,0:T(4,128)} %copy.144), channel_id=1, replica_groups=mesh['dp'=4,'ctx'=4,'uly'=2] {'ctx'}, dimensions={0} | all-to-all | bytes 16777216 | tf_op jit(solution)/shard_map/all_to_all | solution.py:165
  296.7 3.6 %all-to-all-start.4 = ((bf16[2,128,2048]{1,2,0:T(8,128)(2,1)}), bf16[2,128,2048]{1,2,0:T(8,128)(2,1)S(1)}, u32[]{:S(2)}, u32[]{:S(2)}) async-start(bf16[2,128,2048]{1,2,0:T(8,128)(2,1)} %get-tuple-element.41), calls=%async_computation.4 | async-start | bytes 2097152 | tf_op jit(solution)/shard_map/all_to_all | solution.py:173
  300.3 14.1 %fusion.29 = bf16[2,128,1024]{2,0,1:T(2,128)(2,1)S(1)} fusion(f32[4,4,128,1024]{3,1,2,0:T(4,128)} %all_to_all.117, f32[18,128,1024]{2,0,1:T(8,128)} %copy-done.2, s32[4,4,2]{1,2,0:T(2,128)S(1)} %copy-done.5), kind=kOutput, calls=%fused_computation.41 | convolution fusion | flops 50856000 | bytes 9961600 | tf_op jit(solution)/shard_map/csb,csxd->bxd/dot_general | solution.py:166
  315.4 3.4 %all-to-all-start.6 = ((bf16[2,128,512]{2,1,0:T(8,128)(2,1)}), bf16[2,128,512]{2,1,0:T(8,128)(2,1)S(1)}, u32[]{:S(2)}, u32[]{:S(2)}) async-start(bf16[2,128,512]{2,1,0:T(8,128)(2,1)} %copy.146), calls=%async_computation.6 | async-start | bytes 524288 | tf_op jit(solution)/shard_map/all_to_all | solution.py:174
  319.6 4.4 %all-to-all-done.6 = bf16[2,128,512]{2,1,0:T(8,128)(2,1)S(1)} async-done(((bf16[2,128,512]{2,1,0:T(8,128)(2,1)}), bf16[2,128,512]{2,1,0:T(8,128)(2,1)S(1)}, u32[]{:S(2)}, u32[]{:S(2)}) %all-to-all-start.6) | async-done | bytes 262176 | tf_op jit(solution)/shard_map/all_to_all | solution.py:174
  324.0 3.4 %all-to-all-start.7 = ((bf16[2,128,512]{2,1,0:T(8,128)(2,1)}), bf16[2,128,512]{2,1,0:T(8,128)(2,1)S(1)}, u32[]{:S(2)}, u32[]{:S(2)}) async-start(bf16[2,128,512]{2,1,0:T(8,128)(2,1)} %copy.148), calls=%async_computation.7 | async-start | bytes 524288 | tf_op jit(solution)/shard_map/all_to_all | solution.py:175
  329.8 2.8 all-to-all-done.7
  (105 shorter events, 37.6 us)
Async XLA Ops:
  2.6 10.1 %all-to-all-start.2 = ((bf16[128,2,512]{2,0,1:T(8,128)(2,1)}), bf16[128,2,512]{2,0,1:T(8,128)(2,1)S(1)}, u32[]{:S(2)}, u32[]{:S(2)}) async-start(bf16[128,2,512]{2,0,1:T(8,128)(2,1)} %copy.136), calls=%async_computation.2 | async-start | bytes 524288 | tf_op jit(solution)/shard_map/all_to_all | solution.py:80
  12.7 8.6 %all-to-all-start.1 = ((bf16[128,2,512]{2,0,1:T(8,128)(2,1)}), bf16[128,2,512]{2,0,1:T(8,128)(2,1)S(1)}, u32[]{:S(2)}, u32[]{:S(2)}) async-start(bf16[128,2,512]{2,0,1:T(8,128)(2,1)} %copy.133), calls=%async_computation.1 | async-start | bytes 524288 | tf_op jit(solution)/shard_map/all_to_all | solution.py:79
  16.4 8.1 %copy-start.4 = (s32[4,4,2]{1,2,0:T(2,128)}, s32[4,4,2]{1,2,0:T(2,128)S(1)}, u32[]{:S(2)}) copy-start(s32[4,4,2]{1,2,0:T(2,128)S(1)} %convert_reduce_fusion) | copy-start | bytes 388
  30.7 13.2 %collective-permute-start = (bf16[1,4,128,1024]{3,1,2,0:T(4,128)(2,1)}, bf16[1,4,128,1024]{3,1,2,0:T(4,128)(2,1)}, u32[]{:S(2)}, u32[]{:S(2)}) collective-permute-start(bf16[1,4,128,1024]{3,1,2,0:T(4,128)(2,1)} %get-tuple-element.78), channel_id=1, source_target_pairs={{0,2},{2,0},{4,6},{6,4},{1,3},{3,1},{5,7},{7,5},{8,10},{10,8},{12,... | collective-permute-start | bytes 3145736 | tf_op jit(solution)/shard_map/ppermute | solution.py:136
  30.7 27.4 %collective-permute-start.1 = (bf16[1,4,128,1024]{3,1,2,0:T(4,128)(2,1)S(1)}, bf16[1,4,128,1024]{3,1,2,0:T(4,128)(2,1)}, u32[]{:S(2)}, u32[]{:S(2)}) collective-permute-start(bf16[1,4,128,1024]{3,1,2,0:T(4,128)(2,1)S(1)} %get-tuple-element.77), channel_id=1, source_target_pairs={{0,4},{2,6},{4,0},{6,2},{1,5},{3,7},{5,1},{7,3},{8,12},{10,14},{12... | collective-permute-start | bytes 3145736 | tf_op jit(solution)/shard_map/ppermute | solution.py:136
  32.4 46.1 %collective-permute-start.2 = (bf16[1,4,128,1024]{3,1,2,0:T(4,128)(2,1)S(1)}, bf16[1,4,128,1024]{3,1,2,0:T(4,128)(2,1)}, u32[]{:S(2)}, u32[]{:S(2)}) collective-permute-start(bf16[1,4,128,1024]{3,1,2,0:T(4,128)(2,1)S(1)} %get-tuple-element.76), channel_id=1, source_target_pairs={{0,6},{2,4},{4,2},{6,0},{1,7},{3,5},{5,3},{7,1},{8,14},{10,12},{12... | collective-permute-start | bytes 3145736 | tf_op jit(solution)/shard_map/ppermute | solution.py:136
  34.8 18.8 %all-to-all-start = ((bf16[128,2,2048]{0,2,1:T(8,128)(2,1)}), bf16[128,2,2048]{0,2,1:T(8,128)(2,1)}, u32[]{:S(2)}, u32[]{:S(2)}) async-start(bf16[128,2,2048]{0,2,1:T(8,128)(2,1)} %bitcast.31), calls=%async_computation | async-start | bytes 2097152 | tf_op jit(solution)/shard_map/all_to_all | solution.py:77
  53.7 28.9 %all-to-all-start.3 = ((bf16[128,2,2048]{0,2,1:T(8,128)(2,1)}), bf16[128,2,2048]{0,2,1:T(8,128)(2,1)}, u32[]{:S(2)}, u32[]{:S(2)}) async-start(bf16[128,2,2048]{0,2,1:T(8,128)(2,1)} %bitcast.41), calls=%async_computation.3 | async-start | bytes 2097152 | tf_op jit(solution)/shard_map/all_to_all | solution.py:78
  91.4 3.2 copy-start
  97.4 6.1 %copy-start.1 = (f32[4,8,128,128,4]{3,2,4,1,0:T(8,128)S(1)}, f32[4,8,128,128,4]{3,2,4,1,0:T(8,128)}, u32[]{:S(2)}) copy-start(f32[4,8,128,128,4]{3,2,4,1,0:T(8,128)} %copy-done) | copy-start | bytes 25165828 | tf_op jit(solution)/shard_map/while
  107.4 2.6 slice-start
  107.6 3.4 %slice-start.1 = ((s8[8388608]{0:T(1024)(128)(4,1)}), s8[4194304]{0:T(1024)(128)(4,1)S(1)}, s32[]{:S(2)}) async-start(s8[8388608]{0:T(1024)(128)(4,1)} %bitcast.203), calls=%async_computation.9 | async-start | bytes 8388608 | tf_op jit(solution)/shard_map/while
  111.4 3.2 copy-start.3
  124.3 3.2 copy-start
  130.2 6.1 %copy-start.1 = (f32[4,8,128,128,4]{3,2,4,1,0:T(8,128)S(1)}, f32[4,8,128,128,4]{3,2,4,1,0:T(8,128)}, u32[]{:S(2)}) copy-start(f32[4,8,128,128,4]{3,2,4,1,0:T(8,128)} %copy-done) | copy-start | bytes 25165828 | tf_op jit(solution)/shard_map/while
  140.3 2.6 slice-start
  140.5 3.4 %slice-start.1 = ((s8[8388608]{0:T(1024)(128)(4,1)}), s8[4194304]{0:T(1024)(128)(4,1)S(1)}, s32[]{:S(2)}) async-start(s8[8388608]{0:T(1024)(128)(4,1)} %bitcast.203), calls=%async_computation.9 | async-start | bytes 8388608 | tf_op jit(solution)/shard_map/while
  144.3 3.2 copy-start.3
  148.4 8.9 %copy-start.6 = (s32[1,16]{1,0:T(1,128)S(1)}, s32[1,16]{1,0:T(1,128)}, u32[]{:S(2)}) copy-start(s32[1,16]{1,0:T(1,128)} %get-tuple-element.67) | copy-start | bytes 196
  166.9 4.5 %copy-start.2 = (f32[18,128,1024]{2,0,1:T(8,128)}, f32[18,128,1024]{2,0,1:T(8,128)S(1)}, u32[]{:S(2)}) copy-start(f32[18,128,1024]{2,0,1:T(8,128)S(1)} %fusion.35) | copy-start | bytes 28311556
  195.9 104.3 %copy-start.5 = (s32[4,4,2]{1,2,0:T(2,128)S(1)}, s32[4,4,2]{1,2,0:T(2,128)}, u32[]{:S(2)}) copy-start(s32[4,4,2]{1,2,0:T(2,128)} %copy-done.4) | copy-start | bytes 388
  296.7 18.8 %all-to-all-start.4 = ((bf16[2,128,2048]{1,2,0:T(8,128)(2,1)}), bf16[2,128,2048]{1,2,0:T(8,128)(2,1)S(1)}, u32[]{:S(2)}, u32[]{:S(2)}) async-start(bf16[2,128,2048]{1,2,0:T(8,128)(2,1)} %get-tuple-element.41), calls=%async_computation.4 | async-start | bytes 2097152 | tf_op jit(solution)/shard_map/all_to_all | solution.py:173
  315.4 8.6 %all-to-all-start.6 = ((bf16[2,128,512]{2,1,0:T(8,128)(2,1)}), bf16[2,128,512]{2,1,0:T(8,128)(2,1)S(1)}, u32[]{:S(2)}, u32[]{:S(2)}) async-start(bf16[2,128,512]{2,1,0:T(8,128)(2,1)} %copy.146), calls=%async_computation.6 | async-start | bytes 524288 | tf_op jit(solution)/shard_map/all_to_all | solution.py:174
  324.0 8.6 %all-to-all-start.7 = ((bf16[2,128,512]{2,1,0:T(8,128)(2,1)}), bf16[2,128,512]{2,1,0:T(8,128)(2,1)S(1)}, u32[]{:S(2)}, u32[]{:S(2)}) async-start(bf16[2,128,512]{2,1,0:T(8,128)(2,1)} %copy.148), calls=%async_computation.7 | async-start | bytes 524288 | tf_op jit(solution)/shard_map/all_to_all | solution.py:175
